TPU v7x, 32 devices: a whole 2x2x4 slice. The times are simulated.
32 devices in a mesh: row: 4 (over y, x), col: 8 (over z, core).
Axes of the slice: x: 2, y: 2, z: 4, core: 2. Of those that a mesh axis runs over, the one named last changes fastest.
Arguments:
- tokens: bfloat16 [1024, 53248], P(('row', 'col')), may hold values from -6 to 6
- eigvecs: float32 [53248, 2048], P('row', 'col'), may hold values from -0.02734375 to 0.02734375
- eigvals: float32 [2048], P('col'), may hold values from 0.25 to 4
- v_first: float32 [53248, 256], P(('row', 'col')), may hold values from -0.109375 to 0.109375
- v_second: float32 [53248, 256], P(('row', 'col')), may hold values from -0.109375 to 0.109375
- t_first: float32 [256, 256], replicated, may hold values from -0.375 to 0.375
- t_second: float32 [256, 256], replicated, may hold values from -0.375 to 0.375
Outputs:
- whitened: float32 [1024, 2048], P('row', 'col')
All inputs are finite; a program needn't handle non-finite values.
Results may differ from a plain program's by a relative error of at most 0.0029.
Values may be sent and summed in bfloat16 or wider, within the bound.
No kernel may reach another device: no remote copies, remote signals or barrier semaphores. Data moves between devices by JAX's collectives and lax.ppermute only.
A program may use at most 128 MiB of HBM per device.

v0:
```python
import jax
import jax.numpy as jnp
from jax import lax
from jax.sharding import PartitionSpec as P

HIGHEST = lax.Precision.HIGHEST
CHUNKS = 2


def dot32(a, b):
    return jnp.dot(a, b, precision=HIGHEST, preferred_element_type=jnp.float32)


def dot16(a, b):
    return jnp.dot(a, b, preferred_element_type=jnp.float32)


def split(v):
    high = lax.reduce_precision(v, 8, 7)
    return (high.astype(jnp.bfloat16), (v - high).astype(jnp.bfloat16))


def make(rows, cols):
    swap = [(i, i ^ 1) for i in range(cols)]
    groups = [[i for i in range(cols) if i % 2 == core] for core in range(2)]
    half = cols // 2

    def row_sum(x):
        return jnp.sum(lax.all_to_all(x, "row", split_axis=0, concat_axis=0, tiled=True), axis=0)

    def core_sum(parts, core):
        even = jnp.stack(parts[0::2])
        odd = jnp.stack(parts[1::2])
        mine = jnp.where(core == 0, even, odd)
        other = jnp.where(core == 0, odd, even)
        return mine + lax.ppermute(other, "col", swap)

    def z_sum(x):
        got = lax.all_to_all(
            x, "col", split_axis=0, concat_axis=0, tiled=True, axis_index_groups=groups
        )
        return jnp.sum(got, axis=0)

    def per_device(tokens, eigvecs, eigvals, v_first, v_second, t_first, t_second):
        nb = v_first.shape[1]
        core = lax.axis_index("col") % 2
        slab = lax.all_to_all(tokens, ("row", "col"), split_axis=1, concat_axis=0, tiled=True)
        tok = slab.shape[0]
        depth, width = (v_first.shape[0], eigvecs.shape[1])
        high, low = split(jnp.concatenate([v_first, v_second], axis=1))
        along = dot16(slab, high) + dot16(slab, low)
        gram = dot32(v_first.T, v_second)
        packed = jnp.concatenate(
            [
                along.reshape(rows, tok // rows, 2 * nb),
                jnp.broadcast_to(gram.reshape(1, nb // 2, 2 * nb), (rows, nb // 2, 2 * nb)),
            ],
            axis=1,
        )
        packed = packed.reshape(rows * packed.shape[1], 2 * nb)
        packed = lax.psum(lax.psum_scatter(packed, "row", scatter_dimension=0, tiled=True), "col")
        along = packed[: tok // rows]
        gram = packed[tok // rows :].reshape(nb, nb)
        outs = []
        step = width // CHUNKS
        for j in range(CHUNKS):
            piece = (
                eigvecs[:, j * step : (j + 1) * step]
                .astype(jnp.bfloat16)
                .reshape(cols, depth, step)
            )
            piece = lax.all_to_all(piece, "col", split_axis=0, concat_axis=0, tiled=True)
            parts = []
            for s in range(cols):
                w = piece[s]
                p = dot16(slab, w)
                i = dot16(high.T, w) + dot16(low.T, w)
                parts.append(
                    jnp.concatenate(
                        [p.reshape(rows, tok // rows, step), i.reshape(rows, 2 * nb // rows, step)],
                        axis=1,
                    )
                )
            summed = core_sum(parts, core)
            summed = row_sum(jnp.swapaxes(summed, 0, 1))
            summed = z_sum(summed)
            base = summed[: tok // rows]
            inner = summed[tok // rows :]
            inner = lax.all_to_all(
                jnp.broadcast_to(inner[None], (rows, *inner.shape)),
                "row",
                split_axis=0,
                concat_axis=0,
                tiled=True,
            )
            inner = inner.reshape(2 * nb, step)
            m_second = dot32(t_second, inner[nb:])
            m_first = dot32(t_first, inner[:nb] - dot32(gram, m_second))
            scale = lax.rsqrt(eigvals[j * step : (j + 1) * step])
            outs.append(
                (base - dot32(along[:, nb:], m_second) - dot32(along[:, :nb], m_first))
                * scale[None, :]
            )
        return jnp.concatenate(outs, axis=1)

    return per_device


def solution(mesh):
    in_specs = (
        P(("row", "col"), None),
        P("row", "col"),
        P("col"),
        P(("row", "col"), None),
        P(("row", "col"), None),
        P(),
        P(),
    )
    out_specs = P("row", "col")
    body = make(mesh.shape["row"], mesh.shape["col"])
    return jax.shard_map(body, mesh=mesh, in_specs=in_specs, out_specs=out_specs, check_vma=False)
```

profile of v0, /device:TPU:0, one launch (start us, length us, event | category | flops | bytes accessed | tf_op | source)
XLA Modules:
  0.0 556.7 jit_solution(4502269078186748890)
XLA Ops:
  6.5 5.5 convert.4
  14.0 83.4 %all_to_all.59 = bf16[8,1664,128]{2,1,0:T(8,128)(2,1)} all-to-all(bf16[8,1664,128]{2,1,0:T(8,128)(2,1)S(1)} %bitcast.272), channel_id=1, replica_groups=mesh['row'=4,'col'=8] {'col'}, dimensions={0} | all-to-all | bytes 6815744 | tf_op jit(solution)/shard_map/all_to_all | solution.py:72
  97.3 4.5 all-to-all-start.5
  101.8 4.2 copy.39
  116.9 62.0 %all-to-all-done.5 = bf16[8,1664,128]{2,1,0:T(8,128)(2,1)} async-done(((bf16[8,1664,128]{2,1,0:T(8,128)(2,1)}), bf16[8,1664,128]{2,1,0:T(8,128)(2,1)}, u32[]{:S(2)}, u32[]{:S(2)}) %all-to-all-start.5) | async-done | bytes 3407904 | tf_op jit(solution)/shard_map/all_to_all | solution.py:72
  179.0 3.8 all-to-all-start
  226.9 33.8 %all-to-all-done = bf16[32,32,1664]{2,0,1:T(8,128)(2,1)} async-done(((bf16[32,32,1664]{2,0,1:T(8,128)(2,1)}), bf16[32,32,1664]{2,0,1:T(8,128)(2,1)}, u32[]{:S(2)}, u32[]{:S(2)}) %all-to-all-start) | async-done | bytes 3407904 | tf_op jit(solution)/shard_map/all_to_all | solution.py:47
  273.5 3.6 fusion.55
  280.3 3.6 fusion.45
  303.3 3.6 fusion.15
  310.3 3.6 fusion.10
  320.9 3.7 fusion.141
  328.2 6.1 %fusion.140 = f32[512,1024]{1,0:T(8,128)} fusion(bf16[1664,512]{1,0:T(8,128)(2,1)} %copy-done.1, bf16[1024,1664]{1,0:T(8,128)(2,1)} %bitcast.37), kind=kOutput, calls=%fused_computation.194 | convolution fusion | flops 1744830464 | bytes 7208960 | tf_op jit(solution)/shard_map/dot_general | solution.py:15
  338.6 4.7 all-to-all-start.2
  343.3 6.1 %add_bitcast_fusion.2 = f32[1024,512]{0,1:T(8,128)} fusion(f32[512,1024]{1,0:T(8,128)} %fusion.140, bf16[1664,512]{1,0:T(8,128)(2,1)S(1)} %get-tuple-element.7, bf16[1024,1664]{1,0:T(8,128)(2,1)} %bitcast.37), kind=kOutput, calls=%fused_computation.11 | convolution fusion | flops 1745354752 | bytes 9306112 | tf_op jit(solution)/shard_map/dot_general | solution.py:15
  364.9 30.8 %all-to-all-done.2 = f32[4,4,384,128]{3,2,1,0:T(8,128)} async-done(((f32[4,4,384,128]{3,2,1,0:T(8,128)}), f32[4,4,384,128]{3,2,1,0:T(8,128)}, u32[]{:S(2)}, u32[]{:S(2)}) %all-to-all-start.2) | async-done | bytes 3145760 | tf_op jit(solution)/shard_map/all_to_all | solution.py:29
  395.6 3.7 all-to-all-start.6
  402.6 40.4 %all-to-all-done.6 = f32[4,4,384,128]{3,2,1,0:T(8,128)S(1)} async-done(((f32[4,4,384,128]{3,2,1,0:T(8,128)}), f32[4,4,384,128]{3,2,1,0:T(8,128)S(1)}, u32[]{:S(2)}, u32[]{:S(2)}) %all-to-all-start.6) | async-done | bytes 3145760 | tf_op jit(solution)/shard_map/all_to_all | solution.py:29
  443.0 4.2 all-to-all-start.3
  448.3 18.5 %all-to-all-done.3 = f32[4,384,128]{2,1,0:T(8,128)} async-done(((f32[4,384,128]{2,1,0:T(8,128)}), f32[4,384,128]{2,1,0:T(8,128)}, u32[]{:S(2)}, u32[]{:S(2)}) %all-to-all-start.3) | async-done | bytes 786464 | tf_op jit(solution)/shard_map/all_to_all | solution.py:39
  472.3 21.1 %all-to-all-done.7 = f32[4,384,128]{2,1,0:T(8,128)S(1)} async-done(((f32[4,384,128]{2,1,0:T(8,128)}), f32[4,384,128]{2,1,0:T(8,128)S(1)}, u32[]{:S(2)}, u32[]{:S(2)}) %all-to-all-start.7) | async-done | bytes 786464 | tf_op jit(solution)/shard_map/all_to_all | solution.py:39
  497.7 36.4 %all-reduce.2.cloned.1.call-done = f32[384,512]{1,0:T(8,128)} async-done(((f32[384,512]{1,0:T(8,128)}), f32[384,512]{1,0:T(8,128)}) %all-reduce.2.cloned.1.call-update) | async-done | bytes 786448 | tf_op jit(solution)/shard_map/psum | solution.py:61
  536.1 3.6 all-to-all-start.8
  540.2 4.9 all-to-all-done.8
  (221 shorter events, 145.9 us)
Async XLA Ops:
  6.5 533.3 %copy-start = (f32[256,256]{1,0:T(8,128)S(1)}, f32[256,256]{1,0:T(8,128)}, u32[]{:S(2)}) copy-start(f32[256,256]{1,0:T(8,128)} %param.13) | copy-start | bytes 786436
  97.3 81.6 %all-to-all-start.5 = ((bf16[8,1664,128]{2,1,0:T(8,128)(2,1)}), bf16[8,1664,128]{2,1,0:T(8,128)(2,1)}, u32[]{:S(2)}, u32[]{:S(2)}) async-start(bf16[8,1664,128]{2,1,0:T(8,128)(2,1)} %bitcast.271), calls=%async_computation.6 | async-start | bytes 6815744 | tf_op jit(solution)/shard_map/all_to_all | solution.py:72
  108.2 8.0 %copy-start.1 = (bf16[1664,512]{1,0:T(8,128)(2,1)}, bf16[1664,512]{1,0:T(8,128)(2,1)S(1)}, u32[]{:S(2)}) copy-start(bf16[1664,512]{1,0:T(8,128)(2,1)S(1)} %get-tuple-element.8) | copy-start | bytes 5111812
  179.0 81.7 %all-to-all-start = ((bf16[32,32,1664]{2,0,1:T(8,128)(2,1)}), bf16[32,32,1664]{2,0,1:T(8,128)(2,1)}, u32[]{:S(2)}, u32[]{:S(2)}) async-start(bf16[32,32,1664]{2,0,1:T(8,128)(2,1)} %bitcast.270), calls=%async_computation | async-start | bytes 6815744 | tf_op jit(solution)/shard_map/all_to_all | solution.py:47
  273.4 13.7 %copy-start.10 = (f32[1,4,384,128]{3,2,1,0:T(8,128)}, f32[1,4,384,128]{3,2,1,0:T(8,128)S(1)}, u32[]{:S(2)}) copy-start(f32[1,4,384,128]{3,2,1,0:T(8,128)S(1)} %get-tuple-element.25) | copy-start | bytes 2359300
  273.4 13.7 %copy-start.12 = (f32[1,4,384,128]{3,2,1,0:T(8,128)}, f32[1,4,384,128]{3,2,1,0:T(8,128)S(1)}, u32[]{:S(2)}) copy-start(f32[1,4,384,128]{3,2,1,0:T(8,128)S(1)} %get-tuple-element.26) | copy-start | bytes 2359300
  289.6 44.6 %collective-permute-start = (f32[4,4,384,128]{3,2,1,0:T(8,128)}, f32[4,4,384,128]{3,2,1,0:T(8,128)}, u32[]{:S(2)}, u32[]{:S(2)}) collective-permute-start(f32[4,4,384,128]{3,2,1,0:T(8,128)} %fusion.2), channel_id=1, source_target_pairs={{0,1},{1,0},{2,3},{3,2},{4,5},{5,4},{6,7},{7,6},{8,9},{9,8},{10,11... | collective-permute-start | bytes 9437192 | tf_op jit(solution)/shard_map/ppermute | solution.py:36
  302.3 14.9 %copy-start.6 = (f32[1,4,384,128]{3,2,1,0:T(8,128)}, f32[1,4,384,128]{3,2,1,0:T(8,128)S(1)}, u32[]{:S(2)}) copy-start(f32[1,4,384,128]{3,2,1,0:T(8,128)S(1)} %get-tuple-element.15) | copy-start | bytes 2359300
  302.3 14.9 %copy-start.8 = (f32[1,4,384,128]{3,2,1,0:T(8,128)}, f32[1,4,384,128]{3,2,1,0:T(8,128)S(1)}, u32[]{:S(2)}) copy-start(f32[1,4,384,128]{3,2,1,0:T(8,128)S(1)} %get-tuple-element.16) | copy-start | bytes 2359300
  303.3 14.0 %copy-start.14 = (f32[1,4,384,128]{3,2,1,0:T(8,128)}, f32[1,4,384,128]{3,2,1,0:T(8,128)S(1)}, u32[]{:S(2)}) copy-start(f32[1,4,384,128]{3,2,1,0:T(8,128)S(1)} %get-tuple-element.17) | copy-start | bytes 2359300
  303.3 14.0 %copy-start.16 = (f32[1,4,384,128]{3,2,1,0:T(8,128)}, f32[1,4,384,128]{3,2,1,0:T(8,128)S(1)}, u32[]{:S(2)}) copy-start(f32[1,4,384,128]{3,2,1,0:T(8,128)S(1)} %get-tuple-element.18) | copy-start | bytes 2359300
  310.2 7.0 %copy-start.22 = (f32[1,4,384,128]{3,2,1,0:T(8,128)}, f32[1,4,384,128]{3,2,1,0:T(8,128)S(1)}, u32[]{:S(2)}) copy-start(f32[1,4,384,128]{3,2,1,0:T(8,128)S(1)} %get-tuple-element.19) | copy-start | bytes 2359300
  319.6 38.6 %collective-permute-start.1 = (f32[4,4,384,128]{3,2,1,0:T(8,128)}, f32[4,4,384,128]{3,2,1,0:T(8,128)}, u32[]{:S(2)}, u32[]{:S(2)}) collective-permute-start(f32[4,4,384,128]{3,2,1,0:T(8,128)} %fusion.1), channel_id=1, source_target_pairs={{0,1},{1,0},{2,3},{3,2},{4,5},{5,4},{6,7},{7,6},{8,9},{9,8},{10,11... | collective-permute-start | bytes 9437192 | tf_op jit(solution)/shard_map/ppermute | solution.py:36
  338.6 57.1 %all-to-all-start.2 = ((f32[4,4,384,128]{3,2,1,0:T(8,128)}), f32[4,4,384,128]{3,2,1,0:T(8,128)}, u32[]{:S(2)}, u32[]{:S(2)}) async-start(f32[4,4,384,128]{3,2,1,0:T(8,128)} %copy.28), calls=%async_computation.2 | async-start | bytes 6291456 | tf_op jit(solution)/shard_map/all_to_all | solution.py:29
  343.3 127.2 %reduce-scatter.2.cloned.1.call-start = ((), (), s32[]{:S(2)}) async-start(), calls=%async_computation.10 | async-start | bytes 3932160 | tf_op jit(solution)/shard_map/reduce_scatter | solution.py:61
  395.6 47.3 %all-to-all-start.6 = ((f32[4,4,384,128]{3,2,1,0:T(8,128)}), f32[4,4,384,128]{3,2,1,0:T(8,128)S(1)}, u32[]{:S(2)}, u32[]{:S(2)}) async-start(f32[4,4,384,128]{3,2,1,0:T(8,128)} %copy.32), calls=%async_computation.7 | async-start | bytes 6291456 | tf_op jit(solution)/shard_map/all_to_all | solution.py:29
  443.0 23.9 %all-to-all-start.3 = ((f32[4,384,128]{2,1,0:T(8,128)}), f32[4,384,128]{2,1,0:T(8,128)}, u32[]{:S(2)}, u32[]{:S(2)}) async-start(f32[4,384,128]{2,1,0:T(8,128)} %reduce_sum.36), calls=%async_computation.3 | async-start | bytes 1572864 | tf_op jit(solution)/shard_map/all_to_all | solution.py:39
  448.3 49.3 %copy-start.55 = (f32[256]{0:T(256)S(1)}, f32[256]{0:T(256)}, u32[]{:S(2)}) copy-start(f32[256]{0:T(256)} %param.9) | copy-start | bytes 3076
  466.9 26.6 %all-to-all-start.7 = ((f32[4,384,128]{2,1,0:T(8,128)}), f32[4,384,128]{2,1,0:T(8,128)S(1)}, u32[]{:S(2)}, u32[]{:S(2)}) async-start(f32[4,384,128]{2,1,0:T(8,128)} %reduce_sum.38), calls=%async_computation.8 | async-start | bytes 1572864 | tf_op jit(solution)/shard_map/all_to_all | solution.py:39
  470.4 63.8 %all-reduce.2.cloned.1.call-start = ((), (), s32[]{:S(2)}) async-start(), calls=%async_computation.11 | async-start | bytes 1572864 | tf_op jit(solution)/shard_map/psum | solution.py:61
  494.2 41.2 %all-to-all-start.4 = ((f32[4,128,128]{2,1,0:T(8,128)}), f32[4,128,128]{2,1,0:T(8,128)S(1)}, u32[]{:S(2)}, u32[]{:S(2)}) async-start(f32[4,128,128]{2,1,0:T(8,128)} %broadcast_in_dim.10), calls=%async_computation.5 | async-start | bytes 524288 | tf_op jit(solution)/shard_map/all_to_all | solution.py:89
  497.6 48.3 %copy-start.54 = (f32[256,256]{1,0:T(8,128)S(1)}, f32[256,256]{1,0:T(8,128)}, u32[]{:S(2)}) copy-start(f32[256,256]{1,0:T(8,128)} %param.12) | copy-start | bytes 786436
  535.1 12.0 %copy-start.36 = (f32[384,512]{1,0:T(8,128)S(1)}, f32[384,512]{1,0:T(8,128)}, u32[]{:S(2)}) copy-start(f32[384,512]{1,0:T(8,128)} %all-reduce.2.cloned.1.call-done) | copy-start | bytes 2359300
  536.1 9.0 %all-to-all-start.8 = ((f32[4,128,128]{2,1,0:T(8,128)}), f32[4,128,128]{2,1,0:T(8,128)S(1)}, u32[]{:S(2)}, u32[]{:S(2)}) async-start(f32[4,128,128]{2,1,0:T(8,128)} %broadcast_in_dim.11), calls=%async_computation.9 | async-start | bytes 524288 | tf_op jit(solution)/shard_map/all_to_all | solution.py:89
  (44 other events, 152.3 us)
Sparse Core Ops, SparseCore 0:
  358.3 78.5 reduce-scatter.1
  473.5 60.5 all-reduce.1
where the time goes:
time: 564 us; the launch traced here: 557 us
  waiting for transfers between devices  249 us (44%)
  matrix products  122 us (22%)
  blocking collectives  83.4 us (15%)
  starting transfers between devices  32.1 us (6%)
  local copies, waits for them, and re-layouts  31 us (5%)
  other arithmetic  24.5 us (4%)
  between operations  14.8 us (3%)
    dot_general x50, matrix products, dot16(): return jnp.dot(a, b, preferred_element_type=jnp.float32)  114 us
    all_to_all x1, blocking collectives, per_device(): lax.all_to_all(piece, 'col', split_axis=0, concat_axis=0, tiled=True)  83.4 us
    all_to_all x2, waiting for transfers between devices, row_sum(): lax.all_to_all(x, 'row', split_axis=0, concat_axis=0, tiled=True)  71.1 us
    all_to_all x1, waiting for transfers between devices, per_device(): lax.all_to_all(piece, 'col', split_axis=0, concat_axis=0, tiled=True)  62 us
    all_to_all x2, waiting for transfers between devices, z_sum(): lax.all_to_all(x, 'col', split_axis=0, concat_axis=0, tiled=True, axis_in...  39.7 us
    psum x1, waiting for transfers between devices, per_device(): lax.psum(lax.psum_scatter(packed, 'row', scatter_dimension=0, tiled=True)...  36.4 us
    all_to_all x1, waiting for transfers between devices, per_device(): lax.all_to_all(tokens, ('row', 'col'), split_axis=1, concat_axis=0, tiled...  33.8 us
  transfers between devices with their start and end apart: 12, of which 8 were waited for; matrix products, arithmetic and copies ran while one was open for 23% of the time, Pallas kernels for 0%

commit v1 on v0

--- a/solution.py
+++ b/solution.py
@@ -5,6 +5,12 @@
 
 HIGHEST = lax.Precision.HIGHEST
 CHUNKS = 2
+
+
+def add_all(array, mesh_axis):
+    parts = lax.all_gather(array, mesh_axis, axis=0, tiled=False)
+    total = parts.sum(axis=0)
+    return total
 
 
 def dot32(a, b):
@@ -58,7 +64,7 @@
             axis=1,
         )
         packed = packed.reshape(rows * packed.shape[1], 2 * nb)
-        packed = lax.psum(lax.psum_scatter(packed, "row", scatter_dimension=0, tiled=True), "col")
+        packed = add_all(lax.psum_scatter(packed, "row", scatter_dimension=0, tiled=True), "col")
         along = packed[: tok // rows]
         gram = packed[tok // rows :].reshape(nb, nb)
         outs = []

time: 564 us -> 529 us (0.938)
  waiting for transfers between devices: 249 us -> 209 us
    psum x1 -> x0, waiting for transfers between devices: 36.4 us -> none  [per_device(): lax.psum(lax.psum_scatter(packed, 'row', scatter_dimension=0, tiled=True)...]
    unnamed x115 -> x97, local copies, waits for them, and re-layouts: 7.72 us -> 11.5 us
  transfers between devices with their start and end apart: 12 -> 12, of which waited for: 8 -> 8; matrix products, arithmetic and copies ran while one was open for 23% -> 27% of each run, Pallas kernels for 0% -> 0%
where the time goes in v1:
time: 529 us; the launch traced here: 521 us
  waiting for transfers between devices  209 us (40%)
  matrix products  127 us (24%)
  blocking collectives  83.4 us (16%)
  starting transfers between devices  31.6 us (6%)
  local copies, waits for them, and re-layouts  28.3 us (5%)
  other arithmetic  27 us (5%)
  between operations  14.8 us (3%)
    dot_general x50, matrix products, dot16(): return jnp.dot(a, b, preferred_element_type=jnp.float32)  119 us
    all_to_all x1, blocking collectives, per_device(): lax.all_to_all(piece, 'col', split_axis=0, concat_axis=0, tiled=True)  83.4 us
    all_to_all x2, waiting for transfers between devices, row_sum(): lax.all_to_all(x, 'row', split_axis=0, concat_axis=0, tiled=True)  66.3 us
    all_to_all x1, waiting for transfers between devices, per_device(): lax.all_to_all(piece, 'col', split_axis=0, concat_axis=0, tiled=True)  59 us
    all_to_all x1, waiting for transfers between devices, per_device(): lax.all_to_all(tokens, ('row', 'col'), split_axis=1, concat_axis=0, tiled...  36.8 us
    all_to_all x2, waiting for transfers between devices, z_sum(): lax.all_to_all(x, 'col', split_axis=0, concat_axis=0, tiled=True, axis_in...  36.1 us
    unnamed x97, local copies, waits for them, and re-layouts  11.5 us
  transfers between devices with their start and end apart: 12, of which 8 were waited for; matrix products, arithmetic and copies ran while one was open for 27% of the time, Pallas kernels for 0%

profile of v1, /device:TPU:0, one launch (start us, length us, event | category | flops | bytes accessed | tf_op | source)
XLA Modules:
  0.0 520.6 jit_solution(5650583678820597720)
XLA Ops:
  6.5 5.5 %convert.4 = bf16[13312,256]{1,0:T(8,128)(2,1)S(1)} convert(f32[13312,256]{1,0:T(8,128)} %param.8) | non-fusion elementwise | flops 3407872 | bytes 20447232 | tf_op jit(solution)/shard_map/convert.1
  14.1 83.4 %all_to_all.59 = bf16[8,1664,128]{2,1,0:T(8,128)(2,1)} all-to-all(bf16[8,1664,128]{2,1,0:T(8,128)(2,1)S(1)} %bitcast.280), channel_id=1, replica_groups=mesh['row'=4,'col'=8] {'col'}, dimensions={0} | all-to-all | bytes 6815744 | tf_op jit(solution)/shard_map/all_to_all | solution.py:78
  97.5 4.6 all-to-all-start.5
  102.1 4.3 fusion.141
  107.3 3.9 copy.42
  120.2 59.0 %all-to-all-done.5 = bf16[8,1664,128]{2,1,0:T(8,128)(2,1)} async-done(((bf16[8,1664,128]{2,1,0:T(8,128)(2,1)}), bf16[8,1664,128]{2,1,0:T(8,128)(2,1)}, u32[]{:S(2)}, u32[]{:S(2)}) %all-to-all-start.5) | async-done | bytes 3407904 | tf_op jit(solution)/shard_map/all_to_all | solution.py:78
  224.2 36.8 %all-to-all-done = bf16[32,32,1664]{2,0,1:T(8,128)(2,1)} async-done(((bf16[32,32,1664]{2,0,1:T(8,128)(2,1)}), bf16[32,32,1664]{2,0,1:T(8,128)(2,1)}, u32[]{:S(2)}, u32[]{:S(2)}) %all-to-all-start) | async-done | bytes 3407904 | tf_op jit(solution)/shard_map/all_to_all | solution.py:53
  260.9 4.6 fusion.140
  265.5 5.4 %add_bitcast_fusion.2 = f32[1024,512]{0,1:T(8,128)} fusion(f32[512,1024]{1,0:T(8,128)S(1)} %fusion.140, bf16[1664,512]{1,0:T(8,128)(2,1)S(1)} %get-tuple-element.7, bf16[1024,1664]{1,0:T(8,128)(2,1)} %bitcast.37), kind=kOutput, calls=%fused_computation.12 | convolution fusion | flops 1745354752 | bytes 9306112 | tf_op jit(solution)/shard_map/dot_general | solution.py:21
  314.2 3.9 fusion.40
  318.1 3.9 fusion.35
  322.0 3.9 fusion.30
  325.9 3.9 fusion.25
  329.8 3.9 fusion.20
  340.0 4.2 fusion.10
  359.4 4.0 add_bitcast_fusion
  365.2 31.1 %all-to-all-done.2 = f32[4,4,384,128]{3,2,1,0:T(8,128)S(1)} async-done(((f32[4,4,384,128]{3,2,1,0:T(8,128)}), f32[4,4,384,128]{3,2,1,0:T(8,128)S(1)}, u32[]{:S(2)}, u32[]{:S(2)}) %all-to-all-start.2) | async-done | bytes 3145760 | tf_op jit(solution)/shard_map/all_to_all | solution.py:35
  396.4 4.6 all-to-all-start.6
  402.1 35.2 %all-to-all-done.6 = f32[4,4,384,128]{3,2,1,0:T(8,128)} async-done(((f32[4,4,384,128]{3,2,1,0:T(8,128)}), f32[4,4,384,128]{3,2,1,0:T(8,128)}, u32[]{:S(2)}, u32[]{:S(2)}) %all-to-all-start.6) | async-done | bytes 3145760 | tf_op jit(solution)/shard_map/all_to_all | solution.py:35
  443.8 16.6 %all-to-all-done.3 = f32[4,384,128]{2,1,0:T(8,128)S(1)} async-done(((f32[4,384,128]{2,1,0:T(8,128)}), f32[4,384,128]{2,1,0:T(8,128)S(1)}, u32[]{:S(2)}, u32[]{:S(2)}) %all-to-all-start.3) | async-done | bytes 786464 | tf_op jit(solution)/shard_map/all_to_all | solution.py:45
  464.0 19.6 %all-to-all-done.7 = f32[4,384,128]{2,1,0:T(8,128)S(1)} async-done(((f32[4,384,128]{2,1,0:T(8,128)}), f32[4,384,128]{2,1,0:T(8,128)S(1)}, u32[]{:S(2)}, u32[]{:S(2)}) %all-to-all-start.7) | async-done | bytes 786464 | tf_op jit(solution)/shard_map/all_to_all | solution.py:45
  488.0 5.0 all-to-all-done.4
  497.4 5.3 %all-to-all-done.8 = f32[4,128,128]{2,1,0:T(8,128)S(1)} async-done(((f32[4,128,128]{2,1,0:T(8,128)}), f32[4,128,128]{2,1,0:T(8,128)S(1)}, u32[]{:S(2)}, u32[]{:S(2)}) %all-to-all-start.8) | async-done | bytes 262176 | tf_op jit(solution)/shard_map/all_to_all | solution.py:95
  503.5 4.2 copy.40
  (204 shorter events, 149.1 us)
Async XLA Ops:
  6.5 496.2 %copy-start = (f32[256,256]{1,0:T(8,128)S(1)}, f32[256,256]{1,0:T(8,128)}, u32[]{:S(2)}) copy-start(f32[256,256]{1,0:T(8,128)} %param.13) | copy-start | bytes 786436
  97.5 81.7 %all-to-all-start.5 = ((bf16[8,1664,128]{2,1,0:T(8,128)(2,1)}), bf16[8,1664,128]{2,1,0:T(8,128)(2,1)}, u32[]{:S(2)}, u32[]{:S(2)}) async-start(bf16[8,1664,128]{2,1,0:T(8,128)(2,1)} %bitcast.279), calls=%async_computation.6 | async-start | bytes 6815744 | tf_op jit(solution)/shard_map/all_to_all | solution.py:78
  113.5 6.0 %copy-start.1 = (bf16[1664,512]{1,0:T(8,128)(2,1)}, bf16[1664,512]{1,0:T(8,128)(2,1)S(1)}, u32[]{:S(2)}) copy-start(bf16[1664,512]{1,0:T(8,128)(2,1)S(1)} %get-tuple-element.8) | copy-start | bytes 5111812
  179.2 81.7 %all-to-all-start = ((bf16[32,32,1664]{2,0,1:T(8,128)(2,1)}), bf16[32,32,1664]{2,0,1:T(8,128)(2,1)}, u32[]{:S(2)}, u32[]{:S(2)}) async-start(bf16[32,32,1664]{2,0,1:T(8,128)(2,1)} %bitcast.278), calls=%async_computation | async-start | bytes 6815744 | tf_op jit(solution)/shard_map/all_to_all | solution.py:53
  182.8 154.7 %reduce-scatter.2.cloned.1.call-start = ((), (), s32[]{:S(2)}) async-start(), calls=%async_computation.10 | async-start | bytes 3932160 | tf_op jit(solution)/shard_map/reduce_scatter | solution.py:67
  278.6 224.9 %all-gather.3.cloned.1.call-start = ((), (), s32[]{:S(2)}) async-start(), calls=%async_computation.11 | async-start | bytes 7077888 | tf_op jit(solution)/shard_map/all_gather | solution.py:11
  281.2 4.9 copy-start.5
  305.2 6.9 %copy-start.6 = (f32[1,4,384,128]{3,2,1,0:T(8,128)}, f32[1,4,384,128]{3,2,1,0:T(8,128)S(1)}, u32[]{:S(2)}) copy-start(f32[1,4,384,128]{3,2,1,0:T(8,128)S(1)} %get-tuple-element.27) | copy-start | bytes 2359300
  305.2 6.9 %copy-start.8 = (f32[1,4,384,128]{3,2,1,0:T(8,128)}, f32[1,4,384,128]{3,2,1,0:T(8,128)S(1)}, u32[]{:S(2)}) copy-start(f32[1,4,384,128]{3,2,1,0:T(8,128)S(1)} %get-tuple-element.28) | copy-start | bytes 2359300
  314.2 36.5 %collective-permute-start = (f32[4,4,384,128]{3,2,1,0:T(8,128)}, f32[4,4,384,128]{3,2,1,0:T(8,128)}, u32[]{:S(2)}, u32[]{:S(2)}) collective-permute-start(f32[4,4,384,128]{3,2,1,0:T(8,128)} %fusion.2), channel_id=1, source_target_pairs={{0,1},{1,0},{2,3},{3,2},{4,5},{5,4},{6,7},{7,6},{8,9},{9,8},{10,11... | collective-permute-start | bytes 9437192 | tf_op jit(solution)/shard_map/ppermute | solution.py:42
  339.3 8.6 %copy-start.14 = (f32[1,4,384,128]{3,2,1,0:T(8,128)}, f32[1,4,384,128]{3,2,1,0:T(8,128)S(1)}, u32[]{:S(2)}) copy-start(f32[1,4,384,128]{3,2,1,0:T(8,128)S(1)} %get-tuple-element.15) | copy-start | bytes 2359300
  339.3 8.6 %copy-start.15 = (f32[1,4,384,128]{3,2,1,0:T(8,128)}, f32[1,4,384,128]{3,2,1,0:T(8,128)S(1)}, u32[]{:S(2)}) copy-start(f32[1,4,384,128]{3,2,1,0:T(8,128)S(1)} %get-tuple-element.16) | copy-start | bytes 2359300
  339.5 8.4 %copy-start.16 = (f32[1,4,384,128]{3,2,1,0:T(8,128)}, f32[1,4,384,128]{3,2,1,0:T(8,128)S(1)}, u32[]{:S(2)}) copy-start(f32[1,4,384,128]{3,2,1,0:T(8,128)S(1)} %get-tuple-element.17) | copy-start | bytes 2359300
  339.5 8.4 %copy-start.17 = (f32[1,4,384,128]{3,2,1,0:T(8,128)}, f32[1,4,384,128]{3,2,1,0:T(8,128)S(1)}, u32[]{:S(2)}) copy-start(f32[1,4,384,128]{3,2,1,0:T(8,128)S(1)} %get-tuple-element.18) | copy-start | bytes 2359300
  340.0 8.0 %copy-start.18 = (f32[1,4,384,128]{3,2,1,0:T(8,128)}, f32[1,4,384,128]{3,2,1,0:T(8,128)S(1)}, u32[]{:S(2)}) copy-start(f32[1,4,384,128]{3,2,1,0:T(8,128)S(1)} %get-tuple-element.19) | copy-start | bytes 2359300
  340.0 8.0 %copy-start.19 = (f32[1,4,384,128]{3,2,1,0:T(8,128)}, f32[1,4,384,128]{3,2,1,0:T(8,128)S(1)}, u32[]{:S(2)}) copy-start(f32[1,4,384,128]{3,2,1,0:T(8,128)S(1)} %get-tuple-element.20) | copy-start | bytes 2359300
  350.3 9.1 %collective-permute-start.1 = (f32[4,4,384,128]{3,2,1,0:T(8,128)}, f32[4,4,384,128]{3,2,1,0:T(8,128)}, u32[]{:S(2)}, u32[]{:S(2)}) collective-permute-start(f32[4,4,384,128]{3,2,1,0:T(8,128)} %fusion.1), channel_id=1, source_target_pairs={{0,1},{1,0},{2,3},{3,2},{4,5},{5,4},{6,7},{7,6},{8,9},{9,8},{10,11... | collective-permute-start | bytes 9437192 | tf_op jit(solution)/shard_map/ppermute | solution.py:42
  355.7 40.7 %all-to-all-start.2 = ((f32[4,4,384,128]{3,2,1,0:T(8,128)}), f32[4,4,384,128]{3,2,1,0:T(8,128)S(1)}, u32[]{:S(2)}, u32[]{:S(2)}) async-start(f32[4,4,384,128]{3,2,1,0:T(8,128)} %copy.29), calls=%async_computation.2 | async-start | bytes 6291456 | tf_op jit(solution)/shard_map/all_to_all | solution.py:35
  396.4 41.0 %all-to-all-start.6 = ((f32[4,4,384,128]{3,2,1,0:T(8,128)}), f32[4,4,384,128]{3,2,1,0:T(8,128)}, u32[]{:S(2)}, u32[]{:S(2)}) async-start(f32[4,4,384,128]{3,2,1,0:T(8,128)} %copy.33), calls=%async_computation.7 | async-start | bytes 6291456 | tf_op jit(solution)/shard_map/all_to_all | solution.py:35
  437.3 23.1 %all-to-all-start.3 = ((f32[4,384,128]{2,1,0:T(8,128)}), f32[4,384,128]{2,1,0:T(8,128)S(1)}, u32[]{:S(2)}, u32[]{:S(2)}) async-start(f32[4,384,128]{2,1,0:T(8,128)} %reduce_sum.45), calls=%async_computation.3 | async-start | bytes 1572864 | tf_op jit(solution)/shard_map/all_to_all | solution.py:45
  440.8 46.9 %copy-start.45 = (f32[256]{0:T(256)S(1)}, f32[256]{0:T(256)}, u32[]{:S(2)}) copy-start(f32[256]{0:T(256)} %param.9) | copy-start | bytes 3076
  460.4 23.1 %all-to-all-start.7 = ((f32[4,384,128]{2,1,0:T(8,128)}), f32[4,384,128]{2,1,0:T(8,128)S(1)}, u32[]{:S(2)}, u32[]{:S(2)}) async-start(f32[4,384,128]{2,1,0:T(8,128)} %reduce_sum.48), calls=%async_computation.8 | async-start | bytes 1572864 | tf_op jit(solution)/shard_map/all_to_all | solution.py:45
  484.2 8.8 %all-to-all-start.4 = ((f32[4,128,128]{2,1,0:T(8,128)}), f32[4,128,128]{2,1,0:T(8,128)S(1)}, u32[]{:S(2)}, u32[]{:S(2)}) async-start(f32[4,128,128]{2,1,0:T(8,128)} %broadcast_in_dim.10), calls=%async_computation.5 | async-start | bytes 524288 | tf_op jit(solution)/shard_map/all_to_all | solution.py:95
  493.7 8.9 %all-to-all-start.8 = ((f32[4,128,128]{2,1,0:T(8,128)}), f32[4,128,128]{2,1,0:T(8,128)S(1)}, u32[]{:S(2)}, u32[]{:S(2)}) async-start(f32[4,128,128]{2,1,0:T(8,128)} %broadcast_in_dim.11), calls=%async_computation.9 | async-start | bytes 524288 | tf_op jit(solution)/shard_map/all_to_all | solution.py:95
  (34 other events, 91.3 us)
Sparse Core Ops, SparseCore 0:
  278.7 41.5 reduce-scatter.1
  337.7 62.8 all-gather.2
